TPU v7x, 32 devices: a whole 2x2x4 slice. The times are simulated.
32 devices in a mesh: groups: 2 (over y), seq: 4 (over z), adapt: 4 (over x, core).
Axes of the slice: x: 2, y: 2, z: 4, core: 2. Of those that a mesh axis runs over, the one named last changes fastest.
Arguments:
- image: bfloat16 [16, 2048, 3072], P(('groups', 'adapt'), 'seq'), parts along dimension 0, may hold values from -6 to 6
- modulation: float32 [16, 2, 3072], P(('groups', 'adapt')), parts along dimension 0, may hold values from -3 to 3
- query_key_value_weight: bfloat16 [3072, 6144], P(None, 'adapt'), may hold values from -0.109375 to 0.109375
- pooled_down_factor: bfloat16 [16, 3072, 64], P('seq'), may hold values from -0.109375 to 0.109375
- pooled_up_factor: bfloat16 [16, 64, 6144], P('seq', None, 'adapt'), may hold values from -0.75 to 0.75
- request_adapter: int32 [16], P('groups'), parts along dimension 0, may hold values from 0 to 15
- adapter_slot_table: int32 [16], replicated, may hold values from 0 to 15, each once
- row_request: int32 [16], P('groups'), parts along dimension 0, may hold values from 0 to 7, each once
- text_key_value: bfloat16 [16, 512, 2, 2048], P('groups', 'seq', None, 'adapt'), parts along dimension 0, may hold values from -110 to 110
- query_key_gain: float32 [2, 128], replicated, may hold values from 1 to 2.5
Outputs:
- attended: bfloat16 [16, 2048, 2048], P('groups', 'seq', 'adapt'), parts along dimension 0
There are 2 independent parts, one for each index of `groups`. A program takes and returns all parts, laid end to end along the dimension named above; an argument that names none is the same for every part. Nothing has to cross between parts.
All inputs are finite; a program needn't handle non-finite values.
Results may differ from a plain program's by a relative error of at most 0.0049.
The roundings to bfloat16 on the way count: a program that leaves them out, or rounds other values in their place, can miss the bound.
Values may be sent and summed in bfloat16 or wider, within the bound.
A program may use at most 192 MiB of HBM per device.

v0:
```python
import math

import jax
import jax.numpy as jnp
from jax import lax
from jax.sharding import PartitionSpec as P

HEAD_SIZE = 128


def layer_modulate(image, modulation):
    widened = image.astype(jnp.float32)
    centre = widened - jnp.mean(widened, axis=-1, keepdims=True)
    variance = jnp.mean(centre * centre, axis=-1, keepdims=True)
    normed = centre * lax.rsqrt(variance + 1e-06)
    return ((1.0 + modulation[:, 1, None, :]) * normed + modulation[:, 0, None, :]).astype(
        jnp.bfloat16
    )


def rms_scale(values, gain):
    return values * lax.rsqrt(jnp.mean(values * values, axis=-1, keepdims=True) + 1e-06) * gain


def attend_item(operands):
    queries, joined = operands
    key_rows = joined[:, 0]
    value_rows = joined[:, 1]
    query_count = queries.shape[0]
    block = math.gcd(query_count, 512)
    inverse = 1.0 / math.sqrt(queries.shape[-1])
    blocked = queries.reshape(query_count // block, block, queries.shape[-1])

    def one_block(block_rows):
        scores = (
            lax.dot_general(
                block_rows, key_rows, (((1,), (1,)), ((), ())), preferred_element_type=jnp.float32
            )
            * inverse
        )
        highest = jnp.max(scores, axis=-1, keepdims=True)
        weights = jnp.exp(scores - highest)
        weights = weights / jnp.sum(weights, axis=-1, keepdims=True)
        return jnp.dot(
            weights.astype(jnp.bfloat16), value_rows, preferred_element_type=jnp.float32
        ).astype(jnp.bfloat16)

    return lax.map(one_block, blocked).reshape(queries.shape)


def on_device(
    image,
    modulation,
    query_key_value_weight,
    pooled_down_factor,
    pooled_up_factor,
    request_adapter,
    adapter_slot_table,
    row_request,
    text_key_value,
    query_key_gain,
):
    seq_index = lax.axis_index("seq")
    all_requests = request_adapter.shape[0]
    local_pool_slice = pooled_down_factor.shape[0]
    pool_total = adapter_slot_table.shape[0]
    heads_local = query_key_value_weight.shape[1] // (3 * HEAD_SIZE)
    text_local = text_key_value.shape[1]
    modulated = layer_modulate(image, modulation)
    request_match = row_request[:, None] == jnp.arange(all_requests, dtype=jnp.int32)[None, :]
    chosen_ids = jnp.sum(jnp.where(request_match, request_adapter[None, :], 0), axis=1)
    slot_match = chosen_ids[:, None] == jnp.arange(pool_total, dtype=jnp.int32)[None, :]
    slots = jnp.sum(jnp.where(slot_match, adapter_slot_table[None, :], 0), axis=1)
    owned = slots // local_pool_slice == seq_index
    local_match = (slots % local_pool_slice)[:, None] == jnp.arange(
        local_pool_slice, dtype=jnp.int32
    )[None, :]
    slot_picker = (owned[:, None] & local_match).astype(jnp.bfloat16)
    up_terms = jnp.einsum(
        "eq,qfx->efx", slot_picker, pooled_up_factor, preferred_element_type=jnp.float32
    ).astype(jnp.bfloat16)
    down_terms = jnp.einsum(
        "mv,vna->mna", slot_picker, pooled_down_factor, preferred_element_type=jnp.float32
    ).astype(jnp.bfloat16)
    down_fetched, up_fetched = (
        lax.psum(down_terms, "seq").astype(jnp.float32),
        lax.psum(up_terms, "seq").astype(jnp.float32),
    )
    down_fetched = down_fetched.astype(jnp.bfloat16)
    up_fetched = up_fetched.astype(jnp.bfloat16)
    block_rows = lax.all_gather(modulated, "adapt", axis=0, tiled=True)
    shrunk = jnp.einsum(
        "rtd,rdk->rtk", block_rows, down_fetched, preferred_element_type=jnp.float32
    ).astype(jnp.bfloat16)
    frozen = jnp.einsum(
        "rtd,dc->rtc", block_rows, query_key_value_weight, preferred_element_type=jnp.float32
    )
    qkv = frozen + jnp.einsum(
        "rtk,rkc->rtc", shrunk, up_fetched, preferred_element_type=jnp.float32
    )
    token_local = qkv.shape[1]
    qkv = qkv.reshape(all_requests, token_local, heads_local, 3, HEAD_SIZE)
    queries = rms_scale(qkv[:, :, :, 0], query_key_gain[0]).astype(jnp.bfloat16)
    image_keys = rms_scale(qkv[:, :, :, 1], query_key_gain[1]).astype(jnp.bfloat16)
    image_values = qkv[:, :, :, 2].astype(jnp.bfloat16)
    image_pairs = jnp.transpose(jnp.stack([image_keys, image_values], axis=3), (0, 2, 1, 3, 4))
    text_pairs = jnp.transpose(
        text_key_value.reshape(all_requests, text_local, 2, heads_local, HEAD_SIZE), (0, 3, 1, 2, 4)
    )
    joined = jnp.concatenate([image_pairs, text_pairs], axis=2)
    joined = joined.reshape(all_requests * heads_local, token_local + text_local, 2, HEAD_SIZE)
    queries = jnp.transpose(queries, (0, 2, 1, 3)).reshape(
        all_requests * heads_local, token_local, HEAD_SIZE
    )
    query_items, joined_items = (
        lax.all_to_all(queries, "seq", split_axis=0, concat_axis=1, tiled=True),
        lax.all_to_all(joined, "seq", split_axis=0, concat_axis=1, tiled=True),
    )
    attended = lax.map(attend_item, (query_items, joined_items))
    returned = lax.all_to_all(attended, "seq", split_axis=1, concat_axis=0, tiled=True)
    returned = returned.reshape(all_requests, heads_local, token_local, HEAD_SIZE)
    return jnp.transpose(returned, (0, 2, 1, 3)).reshape(
        all_requests, token_local, heads_local * HEAD_SIZE
    )


def solution(mesh):
    in_specs = (
        P(("groups", "adapt"), "seq", None),
        P(("groups", "adapt"), None, None),
        P(None, "adapt"),
        P("seq", None, None),
        P("seq", None, "adapt"),
        P("groups"),
        P(),
        P("groups"),
        P("groups", "seq", None, "adapt"),
        P(),
    )
    out_specs = P("groups", "seq", "adapt")
    return jax.shard_map(
        on_device, mesh=mesh, in_specs=in_specs, out_specs=out_specs, check_vma=False
    )
```

profile of v0, /device:TPU:0, one launch (start us, length us, event | category | flops | bytes accessed | tf_op | source)
XLA Modules:
  0.0 888.3 jit_solution(3175267230559958143)
XLA Ops:
  23.6 9.4 %fusion.13 = bf16[2,512,3072]{2,1,0:T(8,128)(2,1)} fusion(bf16[2,512,3072]{2,1,0:T(8,128)(2,1)} %param.14, f32[2,3072]{1,0:T(2,128)S(1)} %get-tuple-element.83, f32[2,512]{1,0:T(2,128)S(1)} %add_rsqrt_fusion.2, f32[2,512]{1,0:T(2,128)S(1)} %broadcast_multiply_fusion, f32[2,3072]{1,0:T(2,128)S(1)} %get-tuple-element.84), kind=kLoop, calls=%fused_computation.24 | loop fusion | flops 18874368 | bytes 12640256 | tf_op jit(solution)/shard_map/convert_element_type | solution.py:16
  34.2 156.1 %all-reduce.3.cloned.1.call-done = (bf16[8,64,1536]{2,0,1:T(8,128)(2,1)}, bf16[8,3072,64]{1,0,2:T(8,128)(2,1)}) async-done(((bf16[8,64,1536]{2,0,1:T(8,128)(2,1)}, bf16[8,3072,64]{1,0,2:T(8,128)(2,1)}), (bf16[8,64,1536]{2,0,1:T(8,128)(2,1)}, bf16[8,3072,64]{1,0,2:T(8,128)(2,1)})) %all-reduce.3.cloned.1.call-update) | async-done | bytes 4718608 | tf_op jit(solution)/shard_map/psum | solution.py:87
  190.3 23.9 %fusion.18 = f32[8,512,1536]{2,1,0:T(8,128)} fusion(bf16[8,64,1536]{2,0,1:T(8,128)(2,1)} %get-tuple-element.73, bf16[8,512,3072]{2,1,0:T(8,128)(2,1)} %all-gather.2.cloned.1.call-done, bf16[8,3072,64]{1,0,2:T(8,128)(2,1)} %get-tuple-element.74), kind=kOutput, calls=%fused_computation.40 | convolution fusion | flops 2416181248 | bytes 55050240 | tf_op jit(solution)/shard_map/rtk,rkc->rtc/dot_general | solution.py:98
  214.3 47.6 %convolution_add_fusion = f32[8,512,1536]{2,1,0:T(8,128)} fusion(f32[8,512,1536]{2,1,0:T(8,128)} %fusion.18, bf16[8,512,3072]{2,1,0:T(8,128)(2,1)} %all-gather.2.cloned.1.call-done, bf16[3072,1536]{1,0:T(8,128)(2,1)} %param.16), kind=kOutput, calls=%fused_computation.16 | convolution fusion | flops 38660997120 | bytes 84934656 | tf_op jit(solution)/shard_map/rtd,dc->rtc/dot_general | solution.py:95
  261.9 24.7 %copy.49 = f32[8,512,1536]{1,2,0:T(8,128)} copy(f32[8,512,1536]{2,1,0:T(8,128)} %convolution_add_fusion) | data formatting | bytes 50331648 | tf_op jit(solution)/shard_map/add | solution.py:98
  291.2 7.0 fusion.15
  298.2 6.5 copy.50
  327.8 7.0 multiply_convert_fusion
  340.9 9.1 %pad_maximum_fusion = bf16[8,4,640,2,128]{2,4,3,1,0:T(8,128)(2,1)} fusion(bf16[8,4,128,2,128]{2,4,3,1,0:T(8,128)(2,1)} %bitcast.102, bf16[8,4,512,2,128]{2,4,3,1,0:T(8,128)(2,1)} %maximum_bitcast_fusion), kind=kLoop, calls=%fused_computation.25 | loop fusion | flops 20971520 | bytes 20971520 | tf_op jit(solution)/shard_map/concatenate | solution.py:110
  350.1 15.1 %copy.54 = bf16[8,4,640,2,128]{4,2,3,1,0:T(8,128)(2,1)} copy(bf16[8,4,640,2,128]{2,4,3,1,0:T(8,128)(2,1)} %pad_maximum_fusion) | data formatting | bytes 20971520 | tf_op jit(solution)/shard_map/concatenate | solution.py:110
  365.2 38.2 %all-to-all-done = bf16[32,512,128]{2,1,0:T(8,128)(2,1)} async-done(((bf16[32,512,128]{2,1,0:T(8,128)(2,1)}), bf16[32,512,128]{2,1,0:T(8,128)(2,1)}, u32[]{:S(2)}, u32[]{:S(2)}) %all-to-all-start) | async-done | bytes 4194336 | tf_op jit(solution)/shard_map/all_to_all | solution.py:116
  414.0 223.2 %all-to-all-done.1 = bf16[32,640,2,128]{3,1,2,0:T(8,128)(2,1)} async-done(((bf16[32,640,2,128]{3,1,2,0:T(8,128)(2,1)}), bf16[32,640,2,128]{3,1,2,0:T(8,128)(2,1)}, u32[]{:S(2)}, u32[]{:S(2)}) %all-to-all-start.1) | async-done | bytes 10485792 | tf_op jit(solution)/shard_map/all_to_all | solution.py:117
  637.1 9.2 %copy.55 = bf16[8,4,640,2,128]{4,2,1,3,0:T(8,128)(2,1)} copy(bf16[8,4,640,2,128]{4,2,3,0,1:T(8,128)(2,1)} %bitcast.23) | data formatting | bytes 20971520 | tf_op jit(solution)/shard_map/all_to_all | solution.py:117
  646.3 118.3 %while.21 = (s32[]{:T(128)}, bf16[8,2048,128]{2,1,0:T(8,128)(2,1)}, bf16[8,2048,128]{2,1,0:T(8,128)(2,1)}, bf16[8,2560,2,128]{3,1,2,0:T(8,128)(2,1)}, s32[]{:T(128)}, /*index=5*/s32[]{:T(128)}, s32[]{:T(128)}) while((s32[]{:T(128)}, bf16[8,2048,128]{2,1,0:T(8,128)(2,1)}, bf16[8,2048,128]{2,1,0:T(8,128)(2,1)}, ...), condition=%wide.region_13.14_spmd, body=%wide.region_8.13_spmd.sunk | while | flops 680328192 | bytes 24652504 | solution.py:119
  648.9 11.3 %while.22 = (s32[]{:T(128)}, bf16[4,512,128]{2,1,0:T(8,128)(2,1)S(1)}, bf16[4,512,128]{2,1,0:T(8,128)(2,1)S(1)}, bf16[2560,128]{1,0:T(8,128)(2,1)S(1)}, bf16[2560,128]{1,0:T(8,128)(2,1)S(1)}, /*index=5*/s32[]{:T(128)}) while((s32[]{:T(128)}, bf16[4,512,128]{2,1,0:T(8,128)(2,1)S(1)}, bf16[4,512,128]{2,1,0:T(8,128)(2,1)S(1)}, ...), condition=%wide.region_12.12_spmd, body=%wide.region_9.11_spmd.sunk | while | flops 680328192 | bytes 17311820 | solution.py:48
  663.7 11.4 %while.22 = (s32[]{:T(128)}, bf16[4,512,128]{2,1,0:T(8,128)(2,1)S(1)}, bf16[4,512,128]{2,1,0:T(8,128)(2,1)S(1)}, bf16[2560,128]{1,0:T(8,128)(2,1)S(1)}, bf16[2560,128]{1,0:T(8,128)(2,1)S(1)}, /*index=5*/s32[]{:T(128)}) while((s32[]{:T(128)}, bf16[4,512,128]{2,1,0:T(8,128)(2,1)S(1)}, bf16[4,512,128]{2,1,0:T(8,128)(2,1)S(1)}, ...), condition=%wide.region_12.12_spmd, body=%wide.region_9.11_spmd.sunk | while | flops 680328192 | bytes 17311820 | solution.py:48
  678.5 11.4 %while.22 = (s32[]{:T(128)}, bf16[4,512,128]{2,1,0:T(8,128)(2,1)S(1)}, bf16[4,512,128]{2,1,0:T(8,128)(2,1)S(1)}, bf16[2560,128]{1,0:T(8,128)(2,1)S(1)}, bf16[2560,128]{1,0:T(8,128)(2,1)S(1)}, /*index=5*/s32[]{:T(128)}) while((s32[]{:T(128)}, bf16[4,512,128]{2,1,0:T(8,128)(2,1)S(1)}, bf16[4,512,128]{2,1,0:T(8,128)(2,1)S(1)}, ...), condition=%wide.region_12.12_spmd, body=%wide.region_9.11_spmd.sunk | while | flops 680328192 | bytes 17311820 | solution.py:48
  693.3 11.4 %while.22 = (s32[]{:T(128)}, bf16[4,512,128]{2,1,0:T(8,128)(2,1)S(1)}, bf16[4,512,128]{2,1,0:T(8,128)(2,1)S(1)}, bf16[2560,128]{1,0:T(8,128)(2,1)S(1)}, bf16[2560,128]{1,0:T(8,128)(2,1)S(1)}, /*index=5*/s32[]{:T(128)}) while((s32[]{:T(128)}, bf16[4,512,128]{2,1,0:T(8,128)(2,1)S(1)}, bf16[4,512,128]{2,1,0:T(8,128)(2,1)S(1)}, ...), condition=%wide.region_12.12_spmd, body=%wide.region_9.11_spmd.sunk | while | flops 680328192 | bytes 17311820 | solution.py:48
  708.1 11.4 %while.22 = (s32[]{:T(128)}, bf16[4,512,128]{2,1,0:T(8,128)(2,1)S(1)}, bf16[4,512,128]{2,1,0:T(8,128)(2,1)S(1)}, bf16[2560,128]{1,0:T(8,128)(2,1)S(1)}, bf16[2560,128]{1,0:T(8,128)(2,1)S(1)}, /*index=5*/s32[]{:T(128)}) while((s32[]{:T(128)}, bf16[4,512,128]{2,1,0:T(8,128)(2,1)S(1)}, bf16[4,512,128]{2,1,0:T(8,128)(2,1)S(1)}, ...), condition=%wide.region_12.12_spmd, body=%wide.region_9.11_spmd.sunk | while | flops 680328192 | bytes 17311820 | solution.py:48
  722.9 11.4 %while.22 = (s32[]{:T(128)}, bf16[4,512,128]{2,1,0:T(8,128)(2,1)S(1)}, bf16[4,512,128]{2,1,0:T(8,128)(2,1)S(1)}, bf16[2560,128]{1,0:T(8,128)(2,1)S(1)}, bf16[2560,128]{1,0:T(8,128)(2,1)S(1)}, /*index=5*/s32[]{:T(128)}) while((s32[]{:T(128)}, bf16[4,512,128]{2,1,0:T(8,128)(2,1)S(1)}, bf16[4,512,128]{2,1,0:T(8,128)(2,1)S(1)}, ...), condition=%wide.region_12.12_spmd, body=%wide.region_9.11_spmd.sunk | while | flops 680328192 | bytes 17311820 | solution.py:48
  737.6 11.4 %while.22 = (s32[]{:T(128)}, bf16[4,512,128]{2,1,0:T(8,128)(2,1)S(1)}, bf16[4,512,128]{2,1,0:T(8,128)(2,1)S(1)}, bf16[2560,128]{1,0:T(8,128)(2,1)S(1)}, bf16[2560,128]{1,0:T(8,128)(2,1)S(1)}, /*index=5*/s32[]{:T(128)}) while((s32[]{:T(128)}, bf16[4,512,128]{2,1,0:T(8,128)(2,1)S(1)}, bf16[4,512,128]{2,1,0:T(8,128)(2,1)S(1)}, ...), condition=%wide.region_12.12_spmd, body=%wide.region_9.11_spmd.sunk | while | flops 680328192 | bytes 17311820 | solution.py:48
  752.4 11.4 %while.22 = (s32[]{:T(128)}, bf16[4,512,128]{2,1,0:T(8,128)(2,1)S(1)}, bf16[4,512,128]{2,1,0:T(8,128)(2,1)S(1)}, bf16[2560,128]{1,0:T(8,128)(2,1)S(1)}, bf16[2560,128]{1,0:T(8,128)(2,1)S(1)}, /*index=5*/s32[]{:T(128)}) while((s32[]{:T(128)}, bf16[4,512,128]{2,1,0:T(8,128)(2,1)S(1)}, bf16[4,512,128]{2,1,0:T(8,128)(2,1)S(1)}, ...), condition=%wide.region_12.12_spmd, body=%wide.region_9.11_spmd.sunk | while | flops 680328192 | bytes 17311820 | solution.py:48
  769.5 95.4 %all_to_all.51 = bf16[8,2048,128]{2,0,1:T(8,128)(2,1)S(1)} all-to-all(bf16[8,2048,128]{2,0,1:T(8,128)(2,1)S(1)} %copy.56), channel_id=1, replica_groups=mesh['groups'=2,'seq'=4,'adapt'=4] {'seq'}, dimensions={1} | all-to-all | bytes 8388608 | tf_op jit(solution)/shard_map/all_to_all | solution.py:120
  867.8 6.6 copy.59
  (179 shorter events, 193.6 us)
Async XLA Ops:
  7.4 1.8 copy-start
  7.4 182.9 %all-reduce.3.cloned.1.call-start = ((), (), s32[]{:S(2)}) async-start(), calls=%async_computation.4 | async-start | bytes 9437184 | tf_op jit(solution)/shard_map/psum | solution.py:87
  15.2 8.3 copy-start.2
  15.2 175.1 %all-gather.2.cloned.1.call-start = ((), (), s32[]{:S(2)}) async-start(), calls=%async_computation.3 | async-start | bytes 31457280 | tf_op jit(solution)/shard_map/all_gather | solution.py:91
  33.0 0.7 copy-start.4
  304.6 98.7 %all-to-all-start = ((bf16[32,512,128]{2,1,0:T(8,128)(2,1)}), bf16[32,512,128]{2,1,0:T(8,128)(2,1)}, u32[]{:S(2)}, u32[]{:S(2)}) async-start(bf16[32,512,128]{2,1,0:T(8,128)(2,1)} %bitcast.96), calls=%async_computation | async-start | bytes 8388608 | tf_op jit(solution)/shard_map/all_to_all | solution.py:116
  323.1 4.6 copy-start.3
  403.3 233.8 %all-to-all-start.1 = ((bf16[32,640,2,128]{3,1,2,0:T(8,128)(2,1)}), bf16[32,640,2,128]{3,1,2,0:T(8,128)(2,1)}, u32[]{:S(2)}, u32[]{:S(2)}) async-start(bf16[32,640,2,128]{3,1,2,0:T(8,128)(2,1)} %bitcast.94), calls=%async_computation.1 | async-start | bytes 20971520 | tf_op jit(solution)/shard_map/all_to_all | solution.py:117
  867.8 13.0 %copy-start.1 = (bf16[4,3072,64]{1,2,0:T(8,128)(2,1)S(1)}, bf16[4,3072,64]{1,2,0:T(8,128)(2,1)}, u32[]{:S(2)}) copy-start(bf16[4,3072,64]{1,2,0:T(8,128)(2,1)} %param.17) | copy-start | bytes 4718596
Sparse Core Ops, SparseCore 0:
  15.3 174.9 all-reduce.2
Sparse Core Ops, SparseCore 1:
  33.1 157.0 all-gather.1
where the time goes:
time: 891 us; the launch traced here: 888 us
  waiting for transfers between devices  417 us (47%)
  matrix products  141 us (16%)
  local copies, waits for them, and re-layouts  123 us (14%)
  blocking collectives  95.4 us (11%)
  other arithmetic  85 us (10%)
  between operations  15 us (2%)
  starting transfers between devices  11.2 us (1%)
    all_to_all x1, waiting for transfers between devices, on_device(): lax.all_to_all(joined, 'seq', split_axis=0, concat_axis=1, tiled=True)  223 us
    psum x1, waiting for transfers between devices, on_device(): lax.psum(up_terms, 'seq').astype(jnp.float32)  156 us
    all_to_all x1, blocking collectives, on_device(): lax.all_to_all(attended, 'seq', split_axis=1, concat_axis=0, tiled=True)  95.4 us
    dot_general x1, matrix products, on_device(): jnp.einsum('rtd,dc->rtc', block_rows, query_key_value_weight, preferred_e...  47.6 us
    all_to_all x1, waiting for transfers between devices, on_device(): lax.all_to_all(queries, 'seq', split_axis=0, concat_axis=1, tiled=True)  38.2 us
    dot_general x32, matrix products, one_block(): jnp.dot(weights.astype(jnp.bfloat16), value_rows, preferred_element_type=...  33.5 us
    dot_general x32, matrix products, one_block(): lax.dot_general(block_rows, key_rows, (((1,), (1,)), ((), ())), preferred...  29.7 us
    reduce_sum x32, other arithmetic, one_block(): weights = weights / jnp.sum(weights, axis=-1, keepdims=True)  27 us
  transfers between devices with their start and end apart: 4, of which 3 were waited for; matrix products, arithmetic and copies ran while one was open for 9% of the time, Pallas kernels for 0%

commit v1 on v0

--- a/solution.py
+++ b/solution.py
@@ -1,8 +1,11 @@
+import functools
 import math
 
 import jax
 import jax.numpy as jnp
 from jax import lax
+from jax.experimental import pallas as pl
+from jax.experimental.pallas import tpu as pltpu
 from jax.sharding import PartitionSpec as P
 
 HEAD_SIZE = 128
@@ -48,7 +51,7 @@
     return lax.map(one_block, blocked).reshape(queries.shape)
 
 
-def on_device(
+def general_device(
     image,
     modulation,
     query_key_value_weight,
@@ -124,6 +127,355 @@
     )
 
 
+BF16 = jnp.bfloat16
+F32 = jnp.float32
+ANY = pl.BlockSpec(memory_space=pl.ANY)
+
+
+def flipped(index, k):
+    low = 1 - 2 * lax.rem(index, 2) if k % 2 else 0
+    high = 2 - 4 * (index // 2) if k // 2 else 0
+    return index + low + high
+
+
+def move_kernel(
+    mod, text, down, up, tok, txt, down_all, up_all,
+    tok_send, tok_recv, side_send, side_recv, across_send, across_recv, last_send, last_recv,
+    text_send, text_recv, up_send, up_recv, down_send, down_recv, spread_send, spread_recv,
+):
+    s = lax.axis_index("seq")
+    a = lax.axis_index("adapt")
+    x = a // 2
+    c = lax.rem(a, 2)
+    me = s * 4 + a
+    sibling = {"seq": s, "adapt": 2 * x + 1 - c}
+    partner = {"seq": s, "adapt": 2 * (1 - x) + c}
+
+    def remote(source, target, send, recv, device):
+        return pltpu.make_async_remote_copy(
+            src_ref=source, dst_ref=target, send_sem=send, recv_sem=recv,
+            device_id=device, device_id_type=pl.DeviceIdType.MESH,
+        )
+
+    barrier = pltpu.get_barrier_semaphore()
+    for k in range(1, 16):
+        other = lax.rem(me + k, 16)
+        pl.semaphore_signal(
+            barrier, inc=1, device_id={"seq": other // 4, "adapt": lax.rem(other, 4)},
+            device_id_type=pl.DeviceIdType.MESH,
+        )
+    pl.semaphore_wait(barrier, 15)
+
+    for j in range(2):
+        for h in range(2):
+            place = 2 * c + j
+            mine = jnp.logical_and(place == s, c == h)
+            source, target = mod.at[j, h], tok.at[x, s, h]
+            send, recv = tok_send.at[2 * j + h], tok_recv.at[s]
+
+            @pl.when(mine)
+            def _():
+                pltpu.make_async_copy(source, target, recv).start()
+
+            @pl.when(jnp.logical_not(mine))
+            def _():
+                remote(source, target, send, recv, {"seq": place, "adapt": 2 * x + h}).start()
+
+    own = (
+        pltpu.make_async_copy(down.at[:, s], down_all.at[a, s], down_recv.at[s]),
+        pltpu.make_async_copy(up.at[:, s], up_all.at[s], up_recv.at[s]),
+        pltpu.make_async_copy(text.at[:, s], txt.at[:, s], text_recv.at[s]),
+    )
+    for copy in own:
+        copy.start()
+    for k in range(1, 4):
+        place = flipped(s, k)
+        to = {"seq": place, "adapt": a}
+        remote(down.at[:, place], down_all.at[a, s], down_send.at[k], down_recv.at[s], to).start()
+        remote(up.at[:, place], up_all.at[s], up_send.at[k], up_recv.at[s], to).start()
+        remote(text.at[:, place], txt.at[:, s], text_send.at[k], text_recv.at[s], to).start()
+
+    def piece(k):
+        return tok.at[x, flipped(s, k), c]
+
+    def far_piece(k):
+        return tok.at[1 - x, flipped(s, k), c]
+
+    def first(k):
+        return remote(piece(k), piece(k), tok_send.at[0], tok_recv.at[flipped(s, k)], sibling)
+
+    def side(k):
+        return remote(piece(k), piece(k), side_send.at[k], side_recv.at[k], sibling)
+
+    def across(k):
+        return remote(piece(k), piece(k), across_send.at[k], across_recv.at[k], partner)
+
+    def across_in(k):
+        return remote(far_piece(k), far_piece(k), across_send.at[k], across_recv.at[k], partner)
+
+    def last(k):
+        return remote(far_piece(k), far_piece(k), last_send.at[k], last_recv.at[k], sibling)
+
+    def side_in(k):
+        there = tok.at[x, flipped(s, k), 1 - c]
+        return remote(there, there, side_send.at[k], side_recv.at[k], sibling)
+
+    def last_in(k):
+        there = tok.at[1 - x, flipped(s, k), 1 - c]
+        return remote(there, there, last_send.at[k], last_recv.at[k], sibling)
+
+    for k in range(4):
+        first(k).wait_recv()
+        across(k).start()
+        side(k).start()
+        if k > 0:
+            across_in(k - 1).wait_recv()
+            last(k - 1).start()
+    for k in range(4):
+        place = flipped(s, k)
+        remote(
+            down_all.at[a, place], down_all.at[a, place], down_send.at[0], down_recv.at[place], sibling
+        ).wait_recv()
+    for k in range(1, 4):
+        remote(
+            down_all.at[a], down_all.at[a], spread_send.at[k], spread_recv.at[k],
+            {"seq": s, "adapt": flipped(a, k)},
+        ).start()
+    across_in(3).wait_recv()
+    last(3).start()
+
+    for j in range(2):
+        for h in range(2):
+            mine = jnp.logical_and(2 * c + j == s, c == h)
+
+            @pl.when(jnp.logical_not(mine))
+            def _():
+                remote(
+                    mod.at[j, h], tok.at[x, s, h], tok_send.at[2 * j + h], tok_recv.at[s], sibling
+                ).wait_send()
+
+    for k in range(4):
+        side_in(k).wait_recv()
+        last_in(k).wait_recv()
+        side(k).wait_send()
+        across(k).wait_send()
+        last(k).wait_send()
+        place = flipped(s, k)
+        remote(up_all.at[place], up_all.at[place], up_send.at[0], up_recv.at[place], sibling).wait_recv()
+        remote(
+            txt.at[:, place], txt.at[:, place], text_send.at[0], text_recv.at[place], sibling
+        ).wait_recv()
+        if k > 0:
+            remote(down.at[:, place], down_all.at[a, s], down_send.at[k], down_recv.at[s], sibling).wait_send()
+            remote(up.at[:, place], up_all.at[s], up_send.at[k], up_recv.at[s], sibling).wait_send()
+            remote(text.at[:, place], txt.at[:, s], text_send.at[k], text_recv.at[s], sibling).wait_send()
+            other = flipped(a, k)
+            remote(
+                down_all.at[other], down_all.at[other], spread_send.at[k], spread_recv.at[k], sibling
+            ).wait_recv()
+            remote(
+                down_all.at[a], down_all.at[a], spread_send.at[k], spread_recv.at[k], sibling
+            ).wait_send()
+
+
+def project_kernel(tok, weight, down, up, gain, q_out, k_out, v_out):
+    rows = tok[0]
+    shrunk = lax.dot_general(
+        rows, down[0], (((1,), (1,)), ((), ())), preferred_element_type=F32
+    ).astype(BF16)
+    wide = 6 * HEAD_SIZE
+    for part in range(weight.shape[1] // wide):
+        columns = slice(part * wide, (part + 1) * wide)
+        qkv = jnp.dot(rows, weight[:, columns], preferred_element_type=F32)
+        qkv = qkv + jnp.dot(shrunk, up[0, :, columns], preferred_element_type=F32)
+        for h in range(2):
+            head = slice((2 * part + h) * HEAD_SIZE, (2 * part + h + 1) * HEAD_SIZE)
+            q, k, v = (
+                qkv[:, (3 * h + n) * HEAD_SIZE : (3 * h + n + 1) * HEAD_SIZE] for n in range(3)
+            )
+            q_out[0, :, head] = rms_scale(q, gain[0:1, :]).astype(BF16)
+            k_out[0, :, head] = rms_scale(k, gain[1:2, :]).astype(BF16)
+            v_out[0, :, head] = v.astype(BF16)
+
+
+def attend_kernel(rows_at_once, q, k, v, txt, out, held, send, recv):
+    s = lax.axis_index("seq")
+    a = lax.axis_index("adapt")
+    i = pl.program_id(0)
+    token_local = held.shape[1]
+    width = held.shape[2]
+    factor = math.log2(math.e) / math.sqrt(HEAD_SIZE)
+
+    @pl.when(i == 0)
+    def _():
+        barrier = pltpu.get_barrier_semaphore()
+        for n in range(1, 4):
+            pl.semaphore_signal(
+                barrier, inc=1, device_id={"seq": flipped(s, n), "adapt": a},
+                device_id_type=pl.DeviceIdType.MESH,
+            )
+        pl.semaphore_wait(barrier, 3)
+
+    def remote(slot, row, sent, received, place):
+        return pltpu.make_async_remote_copy(
+            src_ref=held.at[slot], dst_ref=out.at[row], send_sem=send.at[sent],
+            recv_sem=recv.at[received], device_id={"seq": place, "adapt": a},
+            device_id_type=pl.DeviceIdType.MESH,
+        )
+
+    def one_block(step, carry):
+        place = jnp.where(step == 3, s, jnp.where(step == 2, flipped(s, 1), jnp.where(step == 1, flipped(s, 3), flipped(s, 2))))
+        slot = i * 4 + step
+        for part in range(token_local // rows_at_once):
+            rows = pl.ds(pl.multiple_of(place * token_local + part * rows_at_once, rows_at_once), rows_at_once)
+            for h in range(width // HEAD_SIZE):
+                head = slice(h * HEAD_SIZE, (h + 1) * HEAD_SIZE)
+                value_head = slice(width + h * HEAD_SIZE, width + (h + 1) * HEAD_SIZE)
+                queries = q[0, rows, head]
+                over_last = (((1,), (1,)), ((), ()))
+                first = lax.dot_general(queries, k[0, :, head], over_last, preferred_element_type=F32)
+                second = lax.dot_general(queries, txt[0, :, head], over_last, preferred_element_type=F32)
+                highest = jnp.maximum(
+                    jnp.max(first, axis=-1, keepdims=True), jnp.max(second, axis=-1, keepdims=True)
+                )
+                first = jnp.exp2((first - highest) * factor)
+                second = jnp.exp2((second - highest) * factor)
+                share = 1.0 / (
+                    jnp.sum(first, axis=-1, keepdims=True) + jnp.sum(second, axis=-1, keepdims=True)
+                )
+                total = jnp.dot((first * share).astype(BF16), v[0, :, head], preferred_element_type=F32)
+                total = total + jnp.dot(
+                    (second * share).astype(BF16), txt[0, :, value_head], preferred_element_type=F32
+                )
+                held[slot, part * rows_at_once : (part + 1) * rows_at_once, head] = total.astype(BF16)
+
+        @pl.when(step == 3)
+        def _():
+            pltpu.make_async_copy(held.at[slot], out.at[i * 4 + s], recv.at[slot]).start()
+
+        @pl.when(step < 3)
+        def _():
+            remote(slot, i * 4 + s, slot, slot, place).start()
+
+        return carry
+
+    lax.fori_loop(0, 4, one_block, 0)
+
+    @pl.when(i == 1)
+    def _():
+        for row in range(2):
+            for step, n in enumerate((2, 3, 1)):
+                slot = row * 4 + step
+                remote(slot, row * 4 + flipped(s, n), slot, slot, flipped(s, n)).wait()
+            slot = row * 4 + 3
+            pltpu.make_async_copy(held.at[slot], out.at[row * 4 + s], recv.at[slot]).wait()
+
+
+def on_device(
+    image,
+    modulation,
+    query_key_value_weight,
+    pooled_down_factor,
+    pooled_up_factor,
+    request_adapter,
+    adapter_slot_table,
+    row_request,
+    text_key_value,
+    query_key_gain,
+):
+    seq_index = lax.axis_index("seq")
+    all_requests = request_adapter.shape[0]
+    pool_local, width, rank = pooled_down_factor.shape
+    pool_total = adapter_slot_table.shape[0]
+    columns = query_key_value_weight.shape[1]
+    head_columns = columns // 3
+    text_local = text_key_value.shape[1]
+    token_local = image.shape[1]
+    tokens = 4 * token_local
+    modulated = layer_modulate(image, modulation)
+    request_match = row_request[:, None] == jnp.arange(all_requests, dtype=jnp.int32)[None, :]
+    chosen_ids = jnp.sum(jnp.where(request_match, request_adapter[None, :], 0), axis=1)
+    slot_match = chosen_ids[:, None] == jnp.arange(pool_total, dtype=jnp.int32)[None, :]
+    slots = jnp.sum(jnp.where(slot_match, adapter_slot_table[None, :], 0), axis=1)
+    owned = slots // pool_local == seq_index
+    local_match = (slots % pool_local)[:, None] == jnp.arange(pool_local, dtype=jnp.int32)[None, :]
+    slot_picker = (owned[:, None] & local_match).astype(BF16)
+    share = width // 4
+    down_part = lax.dynamic_slice_in_dim(
+        pooled_down_factor, lax.axis_index("adapt") * share, share, axis=1
+    )
+    down_terms = jnp.einsum(
+        "mv,vna->man", slot_picker, down_part, preferred_element_type=F32
+    ).astype(BF16)
+    up_terms = jnp.einsum(
+        "eq,qfx->efx", slot_picker, pooled_up_factor, preferred_element_type=F32
+    ).astype(BF16)
+
+    dma = pltpu.SemaphoreType.DMA((4,))
+    tok, txt, down_all, up_all = pl.pallas_call(
+        move_kernel,
+        out_shape=(
+            jax.ShapeDtypeStruct((2, 4, 2, token_local // 2, width), BF16),
+            jax.ShapeDtypeStruct((2, 4, text_local, 2 * head_columns), BF16),
+            jax.ShapeDtypeStruct((4, 4, 2, rank, share), BF16),
+            jax.ShapeDtypeStruct((4, 2, rank, columns), BF16),
+        ),
+        in_specs=[ANY] * 4,
+        out_specs=(ANY,) * 4,
+        scratch_shapes=[dma] * 16,
+        compiler_params=pltpu.CompilerParams(collective_id=0, has_side_effects=True),
+        name="move_tokens",
+    )(
+        modulated.reshape(2, 2, token_local // 2, width),
+        text_key_value.reshape(2, 4, text_local, 2 * head_columns),
+        down_terms.reshape(2, 4, rank, share),
+        up_terms.reshape(2, 4, rank, columns),
+    )
+    tok = tok.reshape(2, tokens, width)
+    txt = txt.reshape(2, 4 * text_local, 2 * head_columns)
+    down = jnp.sum(down_all.astype(F32), axis=1).astype(BF16)
+    down = jnp.transpose(down, (1, 2, 0, 3)).reshape(2, rank, width)
+    up = jnp.sum(up_all.astype(F32), axis=0).astype(BF16)
+
+    block = token_local
+    taken = jax.ShapeDtypeStruct((2, tokens, head_columns), BF16)
+    block_spec = pl.BlockSpec((1, block, head_columns), lambda r, t: (r, t, 0))
+    queries, keys, values = pl.pallas_call(
+        project_kernel,
+        out_shape=(taken,) * 3,
+        grid=(2, tokens // block),
+        in_specs=[
+            pl.BlockSpec((1, block, width), lambda r, t: (r, t, 0)),
+            pl.BlockSpec((width, columns), lambda r, t: (0, 0)),
+            pl.BlockSpec((1, rank, width), lambda r, t: (r, 0, 0)),
+            pl.BlockSpec((1, rank, columns), lambda r, t: (r, 0, 0)),
+            pl.BlockSpec((2, HEAD_SIZE), lambda r, t: (0, 0)),
+        ],
+        out_specs=(block_spec,) * 3,
+        compiler_params=pltpu.CompilerParams(vmem_limit_bytes=56 * 2**20),
+        name="project",
+    )(tok, query_key_value_weight, down, up, query_key_gain)
+
+    whole_spec = pl.BlockSpec((1, tokens, head_columns), lambda r: (r, 0, 0))
+    return pl.pallas_call(
+        functools.partial(attend_kernel, min(256, token_local)),
+        out_shape=jax.ShapeDtypeStruct((all_requests, token_local, head_columns), BF16),
+        grid=(2,),
+        in_specs=[whole_spec] * 3
+        + [pl.BlockSpec((1, 4 * text_local, 2 * head_columns), lambda r: (r, 0, 0))],
+        out_specs=ANY,
+        scratch_shapes=[
+            pltpu.VMEM((8, token_local, head_columns), BF16),
+            pltpu.SemaphoreType.DMA((8,)),
+            pltpu.SemaphoreType.DMA((8,)),
+        ],
+        compiler_params=pltpu.CompilerParams(
+            collective_id=1, has_side_effects=True, vmem_limit_bytes=56 * 2**20
+        ),
+        name="attend",
+    )(queries, keys, values, txt)
+
+
 def solution(mesh):
     in_specs = (
         P(("groups", "adapt"), "seq", None),
@@ -138,6 +490,19 @@
         P(),
     )
     out_specs = P("groups", "seq", "adapt")
+    def chosen(*operands):
+        image, request_adapter = operands[0], operands[5]
+        fits = (
+            mesh.shape["seq"] == 4
+            and mesh.shape["adapt"] == 4
+            and request_adapter.shape[0] == 8
+            and image.shape[0] == 2
+            and operands[2].shape[1] % (6 * HEAD_SIZE) == 0
+            and image.shape[1] % 256 == 0
+            and image.shape[2] % 512 == 0
+        )
+        return (on_device if fits else general_device)(*operands)
+
     return jax.shard_map(
-        on_device, mesh=mesh, in_specs=in_specs, out_specs=out_specs, check_vma=False
-    )
+        chosen, mesh=mesh, in_specs=in_specs, out_specs=out_specs, check_vma=False
+    )

time: 891 us -> 498 us (0.56)
  Pallas kernels: 0 us -> 460 us
  waiting for transfers between devices: 417 us -> 0 us
  matrix products: 141 us -> 1.22 us
  local copies, waits for them, and re-layouts: 123 us -> 12.6 us
  blocking collectives: 95.4 us -> 0 us
  other arithmetic: 85 us -> 21.8 us
  between operations: 15 us -> 0.12 us
  starting transfers between devices: 11.2 us -> 0 us
    pallas_call x0 -> x3, Pallas kernels: none -> 460 us  [the longest x1 242 us: on_device(): pl.pallas_call(move_kernel, out_shape=(jax.ShapeDtypeStruct((2, 4, 2, tok...]
    all_to_all x2 -> x0, waiting for transfers between devices: 261 us -> none  [the longest x1 223 us: on_device(): lax.all_to_all(joined, 'seq', split_axis=0, concat_axis=1, tiled=True)]
    psum x1 -> x0, waiting for transfers between devices: 156 us -> none  [on_device(): lax.psum(up_terms, 'seq').astype(jnp.float32)]
    dot_general x67 -> x1, matrix products: 138 us -> 0.43 us  [on_device(): jnp.einsum('mv,vna->man', slot_picker, down_part, preferred_element_type=...]
    all_to_all x1 -> x0, blocking collectives: 95.4 us -> none  [on_device(): lax.all_to_all(attended, 'seq', split_axis=1, concat_axis=0, tiled=True)]
    reduce_sum x34 -> x2, other arithmetic: 36.2 us -> 4.98 us  [the longest x1 2.5 us: on_device(): up = jnp.sum(up_all.astype(F32), axis=0).astype(BF16)]
    add x1 -> x0, local copies, waits for them, and re-layouts: 24.7 us -> none  [on_device(): frozen + jnp.einsum('rtk,rkc->rtc', shrunk, up_fetched, preferred_element...]
    all_to_all x3 -> x0, local copies, waits for them, and re-layouts: 16.8 us -> none  [the longest x1 9.21 us: on_device(): lax.all_to_all(joined, 'seq', split_axis=0, concat_axis=1, tiled=True)]
  transfers between devices with their start and end apart: 4 -> 0, of which waited for: 3 -> 0; matrix products, arithmetic and copies ran while one was open for 9% -> 0% of each run, Pallas kernels for 0% -> 0%
where the time goes in v1:
time: 498 us; the launch traced here: 495 us
  Pallas kernels  460 us (92%)
  other arithmetic  21.8 us (4%)
  local copies, waits for them, and re-layouts  12.6 us (3%)
    pallas_call x1, Pallas kernels, on_device(): pl.pallas_call(move_kernel, out_shape=(jax.ShapeDtypeStruct((2, 4, 2, tok...  242 us
    pallas_call x1, Pallas kernels, on_device(): pl.pallas_call(functools.partial(attend_kernel, min(256, token_local)), o...  161 us
    pallas_call x1, Pallas kernels, on_device(): pl.pallas_call(project_kernel, out_shape=(taken,) * 3, grid=(2, tokens //...  56.8 us

profile of v1, /device:TPU:0, one launch (start us, length us, event | category | flops | bytes accessed | tf_op | source)
XLA Modules:
  0.0 495.5 jit_solution(15234908614753428754)
XLA Ops:
  0.0 0.0 copy-start
  0.0 1.0 select_reduce_fusion.1
  1.0 1.2 select_reduce_fusion
  2.2 0.0 copy-start.4
  2.2 3.7 convert_reduce_fusion
  6.0 0.0 copy-start.3
  6.0 0.0 copy-done.2
  6.0 1.8 fusion.2
  7.8 0.0 copy-done.4
  7.9 0.0 copy-done
  7.9 0.4 fusion.6
  8.4 1.1 copy.25
  9.4 0.0 copy-done.3
  9.4 0.8 convolution_convert_fusion
  10.2 1.6 copy.27
  11.8 4.4 reshape.69.text
  16.3 9.1 %fusion.5 = bf16[2,512,3072]{2,1,0:T(8,128)(2,1)} fusion(bf16[2,512,3072]{2,1,0:T(8,128)(2,1)} %param.10, f32[2,3072]{1,0:T(2,128)S(1)} %get-tuple-element.21, f32[2,512]{1,0:T(2,128)S(1)} %add_rsqrt_fusion, f32[2,512]{1,0:T(2,128)S(1)} %broadcast_multiply_fusion, f32[2,3072]{1,0:T(2,128)S(1)} %get-tuple-element.22), kind=kLoop, calls=%fused_computation.7 | loop fusion | flops 18874368 | bytes 12640256 | tf_op jit(solution)/shard_map/convert_element_type | solution.py:19
  25.4 241.7 %move_tokens.1 = (bf16[2,4,2,256,3072]{4,3,2,1,0:T(8,128)(2,1)}, bf16[2,4,128,1024]{3,2,1,0:T(8,128)(2,1)}, bf16[4,4,2,64,768]{4,3,2,1,0:T(8,128)(2,1)}, bf16[4,2,64,1536]{3,2,1,0:T(8,128)(2,1)}) custom-call(bf16[2,2,256,3072]{3,2,1,0:T(8,128)(2,1)} %bitcast.19, bf16[2,4,128,1024]{3,2,1,0:T(8,128)(2,1)} %reshape.69.text, bf16[2,4,64,768]{3,2,1,0:T(8,128)(2,1)} %bitcast.22, ...), custom_call_target="tpu_custom_call" | custom-call | tf_op jit(solution)/shard_map/move_tokens/pallas_call | solution.py:415
  267.0 2.5 reduce_sum.65.up
  269.5 2.5 reduce_sum.64
  272.0 1.0 copy.32
  273.0 56.8 %project.1 = (bf16[2,2048,512]{2,1,0:T(8,128)(2,1)}, bf16[2,2048,512]{2,1,0:T(8,128)(2,1)}, bf16[2,2048,512]{2,1,0:T(8,128)(2,1)}) custom-call(bf16[2,2048,3072]{2,1,0:T(8,128)(2,1)} %bitcast.18, bf16[3072,1536]{1,0:T(8,128)(2,1)} %weight.1, bf16[2,64,3072]{2,1,0:T(8,128)(2,1)} %bitcast.23, bf16[2,64,1536]{2,1,0:T(8,128)(2,1)} %reduce_sum.65.up, f32[2,128]{1,0:T(2,128)} %gain.1), custom_call_target="tpu_custom_call" | custom-call | tf_op jit(solution)/shard_map/project/pallas_call | solution.py:443
  329.8 161.2 %attend.1 = bf16[8,512,512]{2,1,0:T(8,128)(2,1)} custom-call(bf16[2,2048,512]{2,1,0:T(8,128)(2,1)} %get-tuple-element.15.q, bf16[2,2048,512]{2,1,0:T(8,128)(2,1)} %get-tuple-element.16.k, bf16[2,2048,512]{2,1,0:T(8,128)(2,1)} %get-tuple-element.17.v, bf16[2,512,1024]{2,1,0:T(8,128)(2,1)} %bitcast.24), custom_call_target="tpu_custom_call" | custom-call | tf_op jit(solution)/shard_map/attend/pallas_call | solution.py:460
  491.0 4.5 copy.40
  (10 shorter events, 0.2 us)
Async XLA Ops:
  0.0 7.9 %copy-start = (bf16[4,3072,64]{1,2,0:T(8,128)(2,1)S(1)}, bf16[4,3072,64]{1,2,0:T(8,128)(2,1)}, u32[]{:S(2)}) copy-start(bf16[4,3072,64]{1,2,0:T(8,128)(2,1)} %param.13) | copy-start | bytes 4718596
  0.0 6.0 %copy-start.2 = (bf16[2,512,3072]{2,1,0:T(8,128)(2,1)S(1)}, bf16[2,512,3072]{2,1,0:T(8,128)(2,1)}, u32[]{:S(2)}) copy-start(bf16[2,512,3072]{2,1,0:T(8,128)(2,1)} %param.10) | copy-start | bytes 18874372
  2.2 5.6 %copy-start.4 = (f32[2,2,3072]{2,1,0:T(2,128)S(1)}, f32[2,2,3072]{2,1,0:T(2,128)}, u32[]{:S(2)}) copy-start(f32[2,2,3072]{2,1,0:T(2,128)} %param.11) | copy-start | bytes 147460
  6.0 3.5 copy-start.3
  329.8 165.7 %copy-start.1 = (bf16[4,3072,64]{1,2,0:T(8,128)(2,1)S(1)}, bf16[4,3072,64]{1,2,0:T(8,128)(2,1)}, u32[]{:S(2)}) copy-start(bf16[4,3072,64]{1,2,0:T(8,128)(2,1)} %param.13) | copy-start | bytes 4718596

commit v2 on v1

--- a/solution.py
+++ b/solution.py
@@ -128,6 +128,7 @@
 
 
 BF16 = jnp.bfloat16
+ROUNDS = 4
 F32 = jnp.float32
 ANY = pl.BlockSpec(memory_space=pl.ANY)
 
@@ -139,9 +140,9 @@
 
 
 def move_kernel(
-    mod, text, down, up, tok, txt, down_all, up_all,
+    mod, down, up, tok, down_all, up_all,
     tok_send, tok_recv, side_send, side_recv, across_send, across_recv, last_send, last_recv,
-    text_send, text_recv, up_send, up_recv, down_send, down_recv, spread_send, spread_recv,
+    up_send, up_recv, down_send, down_recv, spread_send, spread_recv,
 ):
     s = lax.axis_index("seq")
     a = lax.axis_index("adapt")
@@ -166,25 +167,43 @@
         )
     pl.semaphore_wait(barrier, 15)
 
-    for j in range(2):
-        for h in range(2):
-            place = 2 * c + j
-            mine = jnp.logical_and(place == s, c == h)
-            source, target = mod.at[j, h], tok.at[x, s, h]
-            send, recv = tok_send.at[2 * j + h], tok_recv.at[s]
-
-            @pl.when(mine)
-            def _():
-                pltpu.make_async_copy(source, target, recv).start()
-
-            @pl.when(jnp.logical_not(mine))
-            def _():
-                remote(source, target, send, recv, {"seq": place, "adapt": 2 * x + h}).start()
-
+    def handed(n, j, h):
+        place = 2 * c + j
+        mine = jnp.logical_and(place == s, c == h)
+        recv = tok_recv.at[n, s]
+        source, target = mod.at[j, h, n], tok.at[x, s, h, n]
+        away = remote(
+            source, target, tok_send.at[n, 2 * j + h], recv, {"seq": place, "adapt": 2 * x + h}
+        )
+        return mine, away, pltpu.make_async_copy(source, target, recv)
+
+    def start_round(n):
+        for j in range(2):
+            for h in range(2):
+                mine, away, here = handed(n, j, h)
+
+                @pl.when(mine)
+                def _():
+                    here.start()
+
+                @pl.when(jnp.logical_not(mine))
+                def _():
+                    away.start()
+
+    def end_round(n):
+        for j in range(2):
+            for h in range(2):
+                mine, away, _ = handed(n, j, h)
+
+                @pl.when(jnp.logical_not(mine))
+                def _():
+                    away.wait_send()
+
+    start_round(0)
+    start_round(1)
     own = (
         pltpu.make_async_copy(down.at[:, s], down_all.at[a, s], down_recv.at[s]),
         pltpu.make_async_copy(up.at[:, s], up_all.at[s], up_recv.at[s]),
-        pltpu.make_async_copy(text.at[:, s], txt.at[:, s], text_recv.at[s]),
     )
     for copy in own:
         copy.start()
@@ -193,44 +212,50 @@
         to = {"seq": place, "adapt": a}
         remote(down.at[:, place], down_all.at[a, s], down_send.at[k], down_recv.at[s], to).start()
         remote(up.at[:, place], up_all.at[s], up_send.at[k], up_recv.at[s], to).start()
-        remote(text.at[:, place], txt.at[:, s], text_send.at[k], text_recv.at[s], to).start()
-
-    def piece(k):
-        return tok.at[x, flipped(s, k), c]
-
-    def far_piece(k):
-        return tok.at[1 - x, flipped(s, k), c]
-
-    def first(k):
-        return remote(piece(k), piece(k), tok_send.at[0], tok_recv.at[flipped(s, k)], sibling)
-
-    def side(k):
-        return remote(piece(k), piece(k), side_send.at[k], side_recv.at[k], sibling)
-
-    def across(k):
-        return remote(piece(k), piece(k), across_send.at[k], across_recv.at[k], partner)
-
-    def across_in(k):
-        return remote(far_piece(k), far_piece(k), across_send.at[k], across_recv.at[k], partner)
-
-    def last(k):
-        return remote(far_piece(k), far_piece(k), last_send.at[k], last_recv.at[k], sibling)
-
-    def side_in(k):
-        there = tok.at[x, flipped(s, k), 1 - c]
-        return remote(there, there, side_send.at[k], side_recv.at[k], sibling)
-
-    def last_in(k):
-        there = tok.at[1 - x, flipped(s, k), 1 - c]
-        return remote(there, there, last_send.at[k], last_recv.at[k], sibling)
-
-    for k in range(4):
-        first(k).wait_recv()
-        across(k).start()
-        side(k).start()
-        if k > 0:
-            across_in(k - 1).wait_recv()
-            last(k - 1).start()
+
+    def piece(n, k):
+        return tok.at[x, flipped(s, k), c, n]
+
+    def far_piece(n, k):
+        return tok.at[1 - x, flipped(s, k), c, n]
+
+    def first(n, k):
+        return remote(piece(n, k), piece(n, k), tok_send.at[n, 0], tok_recv.at[n, flipped(s, k)], sibling)
+
+    def side(n, k):
+        return remote(piece(n, k), piece(n, k), side_send.at[n, k], side_recv.at[n, k], sibling)
+
+    def across(n, k):
+        return remote(piece(n, k), piece(n, k), across_send.at[n, k], across_recv.at[n, k], partner)
+
+    def across_in(n, k):
+        return remote(
+            far_piece(n, k), far_piece(n, k), across_send.at[n, k], across_recv.at[n, k], partner
+        )
+
+    def last(n, k):
+        return remote(far_piece(n, k), far_piece(n, k), last_send.at[n, k], last_recv.at[n, k], sibling)
+
+    def side_in(n, k):
+        there = tok.at[x, flipped(s, k), 1 - c, n]
+        return remote(there, there, side_send.at[n, k], side_recv.at[n, k], sibling)
+
+    def last_in(n, k):
+        there = tok.at[1 - x, flipped(s, k), 1 - c, n]
+        return remote(there, there, last_send.at[n, k], last_recv.at[n, k], sibling)
+
+    for n in range(ROUNDS):
+        for k in range(4):
+            first(n, k).wait_recv()
+            across(n, k).start()
+            side(n, k).start()
+        end_round(n)
+        if n + 2 < ROUNDS:
+            start_round(n + 2)
+        if n > 0:
+            for k in range(4):
+                across_in(n - 1, k).wait_recv()
+                last(n - 1, k).start()
     for k in range(4):
         place = flipped(s, k)
         remote(
@@ -241,34 +266,22 @@
             down_all.at[a], down_all.at[a], spread_send.at[k], spread_recv.at[k],
             {"seq": s, "adapt": flipped(a, k)},
         ).start()
-    across_in(3).wait_recv()
-    last(3).start()
-
-    for j in range(2):
-        for h in range(2):
-            mine = jnp.logical_and(2 * c + j == s, c == h)
-
-            @pl.when(jnp.logical_not(mine))
-            def _():
-                remote(
-                    mod.at[j, h], tok.at[x, s, h], tok_send.at[2 * j + h], tok_recv.at[s], sibling
-                ).wait_send()
-
     for k in range(4):
-        side_in(k).wait_recv()
-        last_in(k).wait_recv()
-        side(k).wait_send()
-        across(k).wait_send()
-        last(k).wait_send()
+        across_in(ROUNDS - 1, k).wait_recv()
+        last(ROUNDS - 1, k).start()
+
+    for k in range(4):
+        for n in range(ROUNDS):
+            side_in(n, k).wait_recv()
+            last_in(n, k).wait_recv()
+            side(n, k).wait_send()
+            across(n, k).wait_send()
+            last(n, k).wait_send()
         place = flipped(s, k)
         remote(up_all.at[place], up_all.at[place], up_send.at[0], up_recv.at[place], sibling).wait_recv()
-        remote(
-            txt.at[:, place], txt.at[:, place], text_send.at[0], text_recv.at[place], sibling
-        ).wait_recv()
         if k > 0:
             remote(down.at[:, place], down_all.at[a, s], down_send.at[k], down_recv.at[s], sibling).wait_send()
             remote(up.at[:, place], up_all.at[s], up_send.at[k], up_recv.at[s], sibling).wait_send()
-            remote(text.at[:, place], txt.at[:, s], text_send.at[k], text_recv.at[s], sibling).wait_send()
             other = flipped(a, k)
             remote(
                 down_all.at[other], down_all.at[other], spread_send.at[k], spread_recv.at[k], sibling
@@ -278,7 +291,37 @@
             ).wait_send()
 
 
-def project_kernel(tok, weight, down, up, gain, q_out, k_out, v_out):
+def project_kernel(
+    tok, weight, down, up, gain, text, q_out, k_out, v_out, txt, text_send, text_recv
+):
+    s = lax.axis_index("seq")
+    a = lax.axis_index("adapt")
+    r = pl.program_id(0)
+    t = pl.program_id(1)
+
+    def text_copy(k):
+        place = flipped(s, k)
+        return pltpu.make_async_remote_copy(
+            src_ref=text.at[:, place], dst_ref=txt.at[:, s], send_sem=text_send.at[k],
+            recv_sem=text_recv.at[k], device_id={"seq": place, "adapt": a},
+            device_id_type=pl.DeviceIdType.MESH,
+        )
+
+    own_text = pltpu.make_async_copy(text.at[:, s], txt.at[:, s], text_recv.at[0])
+
+    @pl.when(jnp.logical_and(r == 0, t == 0))
+    def _():
+        barrier = pltpu.get_barrier_semaphore()
+        for n in range(1, 4):
+            pl.semaphore_signal(
+                barrier, inc=1, device_id={"seq": flipped(s, n), "adapt": a},
+                device_id_type=pl.DeviceIdType.MESH,
+            )
+        pl.semaphore_wait(barrier, 3)
+        for k in (2, 3, 1):
+            text_copy(k).start()
+        own_text.start()
+
     rows = tok[0]
     shrunk = lax.dot_general(
         rows, down[0], (((1,), (1,)), ((), ())), preferred_element_type=F32
@@ -297,6 +340,12 @@
             k_out[0, :, head] = rms_scale(k, gain[1:2, :]).astype(BF16)
             v_out[0, :, head] = v.astype(BF16)
 
+    @pl.when(jnp.logical_and(r == pl.num_programs(0) - 1, t == pl.num_programs(1) - 1))
+    def _():
+        for k in (2, 3, 1):
+            text_copy(k).wait()
+        own_text.wait()
+
 
 def attend_kernel(rows_at_once, q, k, v, txt, out, held, send, recv):
     s = lax.axis_index("seq")
@@ -326,28 +375,42 @@
     def one_block(step, carry):
         place = jnp.where(step == 3, s, jnp.where(step == 2, flipped(s, 1), jnp.where(step == 1, flipped(s, 3), flipped(s, 2))))
         slot = i * 4 + step
-        for part in range(token_local // rows_at_once):
-            rows = pl.ds(pl.multiple_of(place * token_local + part * rows_at_once, rows_at_once), rows_at_once)
-            for h in range(width // HEAD_SIZE):
-                head = slice(h * HEAD_SIZE, (h + 1) * HEAD_SIZE)
-                value_head = slice(width + h * HEAD_SIZE, width + (h + 1) * HEAD_SIZE)
-                queries = q[0, rows, head]
-                over_last = (((1,), (1,)), ((), ()))
-                first = lax.dot_general(queries, k[0, :, head], over_last, preferred_element_type=F32)
-                second = lax.dot_general(queries, txt[0, :, head], over_last, preferred_element_type=F32)
-                highest = jnp.maximum(
-                    jnp.max(first, axis=-1, keepdims=True), jnp.max(second, axis=-1, keepdims=True)
+        work = [
+            (part, h) for part in range(token_local // rows_at_once) for h in range(width // HEAD_SIZE)
+        ]
+
+        def scores(part, h):
+            rows = pl.ds(
+                pl.multiple_of(place * token_local + part * rows_at_once, rows_at_once), rows_at_once
+            )
+            head = slice(h * HEAD_SIZE, (h + 1) * HEAD_SIZE)
+            return tuple(
+                lax.dot_general(
+                    q[0, rows, head], key_rows, (((1,), (1,)), ((), ())), preferred_element_type=F32
                 )
-                first = jnp.exp2((first - highest) * factor)
-                second = jnp.exp2((second - highest) * factor)
-                share = 1.0 / (
-                    jnp.sum(first, axis=-1, keepdims=True) + jnp.sum(second, axis=-1, keepdims=True)
-                )
-                total = jnp.dot((first * share).astype(BF16), v[0, :, head], preferred_element_type=F32)
-                total = total + jnp.dot(
-                    (second * share).astype(BF16), txt[0, :, value_head], preferred_element_type=F32
-                )
-                held[slot, part * rows_at_once : (part + 1) * rows_at_once, head] = total.astype(BF16)
+                for key_rows in (k[0, :, head], txt[0, :, head])
+            )
+
+        ready = scores(*work[0])
+        for n, (part, h) in enumerate(work):
+            first, second = ready
+            if n + 1 < len(work):
+                ready = scores(*work[n + 1])
+            head = slice(h * HEAD_SIZE, (h + 1) * HEAD_SIZE)
+            value_head = slice(width + h * HEAD_SIZE, width + (h + 1) * HEAD_SIZE)
+            highest = jnp.maximum(
+                jnp.max(first, axis=-1, keepdims=True), jnp.max(second, axis=-1, keepdims=True)
+            )
+            first = jnp.exp2((first - highest) * factor)
+            second = jnp.exp2((second - highest) * factor)
+            share = 1.0 / (
+                jnp.sum(first, axis=-1, keepdims=True) + jnp.sum(second, axis=-1, keepdims=True)
+            )
+            total = jnp.dot((first * share).astype(BF16), v[0, :, head], preferred_element_type=F32)
+            total = total + jnp.dot(
+                (second * share).astype(BF16), txt[0, :, value_head], preferred_element_type=F32
+            )
+            held[slot, part * rows_at_once : (part + 1) * rows_at_once, head] = total.astype(BF16)
 
         @pl.when(step == 3)
         def _():
@@ -412,27 +475,24 @@
     ).astype(BF16)
 
     dma = pltpu.SemaphoreType.DMA((4,))
-    tok, txt, down_all, up_all = pl.pallas_call(
+    tok, down_all, up_all = pl.pallas_call(
         move_kernel,
         out_shape=(
-            jax.ShapeDtypeStruct((2, 4, 2, token_local // 2, width), BF16),
-            jax.ShapeDtypeStruct((2, 4, text_local, 2 * head_columns), BF16),
+            jax.ShapeDtypeStruct((2, 4, 2, ROUNDS, token_local // (2 * ROUNDS), width), BF16),
             jax.ShapeDtypeStruct((4, 4, 2, rank, share), BF16),
             jax.ShapeDtypeStruct((4, 2, rank, columns), BF16),
         ),
-        in_specs=[ANY] * 4,
-        out_specs=(ANY,) * 4,
-        scratch_shapes=[dma] * 16,
+        in_specs=[ANY] * 3,
+        out_specs=(ANY,) * 3,
+        scratch_shapes=[pltpu.SemaphoreType.DMA((ROUNDS, 4))] * 8 + [dma] * 6,
         compiler_params=pltpu.CompilerParams(collective_id=0, has_side_effects=True),
         name="move_tokens",
     )(
-        modulated.reshape(2, 2, token_local // 2, width),
-        text_key_value.reshape(2, 4, text_local, 2 * head_columns),
+        modulated.reshape(2, 2, ROUNDS, token_local // (2 * ROUNDS), width),
         down_terms.reshape(2, 4, rank, share),
         up_terms.reshape(2, 4, rank, columns),
     )
     tok = tok.reshape(2, tokens, width)
-    txt = txt.reshape(2, 4 * text_local, 2 * head_columns)
     down = jnp.sum(down_all.astype(F32), axis=1).astype(BF16)
     down = jnp.transpose(down, (1, 2, 0, 3)).reshape(2, rank, width)
     up = jnp.sum(up_all.astype(F32), axis=0).astype(BF16)
@@ -440,9 +500,10 @@
     block = token_local
     taken = jax.ShapeDtypeStruct((2, tokens, head_columns), BF16)
     block_spec = pl.BlockSpec((1, block, head_columns), lambda r, t: (r, t, 0))
-    queries, keys, values = pl.pallas_call(
+    queries, keys, values, txt = pl.pallas_call(
         project_kernel,
-        out_shape=(taken,) * 3,
+        out_shape=(taken,) * 3
+        + (jax.ShapeDtypeStruct((2, 4, text_local, 2 * head_columns), BF16),),
         grid=(2, tokens // block),
         in_specs=[
             pl.BlockSpec((1, block, width), lambda r, t: (r, t, 0)),
@@ -450,15 +511,23 @@
             pl.BlockSpec((1, rank, width), lambda r, t: (r, 0, 0)),
             pl.BlockSpec((1, rank, columns), lambda r, t: (r, 0, 0)),
             pl.BlockSpec((2, HEAD_SIZE), lambda r, t: (0, 0)),
+            ANY,
         ],
-        out_specs=(block_spec,) * 3,
-        compiler_params=pltpu.CompilerParams(vmem_limit_bytes=56 * 2**20),
+        out_specs=(block_spec,) * 3 + (ANY,),
+        scratch_shapes=[dma] * 2,
+        compiler_params=pltpu.CompilerParams(
+            collective_id=2, has_side_effects=True, vmem_limit_bytes=56 * 2**20
+        ),
         name="project",
-    )(tok, query_key_value_weight, down, up, query_key_gain)
+    )(
+        tok, query_key_value_weight, down, up, query_key_gain,
+        text_key_value.reshape(2, 4, text_local, 2 * head_columns),
+    )
+    txt = txt.reshape(2, 4 * text_local, 2 * head_columns)
 
     whole_spec = pl.BlockSpec((1, tokens, head_columns), lambda r: (r, 0, 0))
     return pl.pallas_call(
-        functools.partial(attend_kernel, min(256, token_local)),
+        functools.partial(attend_kernel, math.gcd(512, token_local)),
         out_shape=jax.ShapeDtypeStruct((all_requests, token_local, head_columns), BF16),
         grid=(2,),
         in_specs=[whole_spec] * 3

time: 498 us -> 458 us (0.920); the launches traced: 495 us -> 450 us
  Pallas kernels: 460 us -> 414 us
    pallas_call x3, Pallas kernels: 460 us -> 414 us  [the longest x1 252 us: on_device(): pl.pallas_call(move_kernel, out_shape=(jax.ShapeDtypeStruct((2, 4, 2, ROU...]
where the time goes in v2:
time: 458 us; the launch traced here: 450 us
  Pallas kernels  414 us (90%)
  other arithmetic  21.8 us (5%)
  local copies, waits for them, and re-layouts  12.7 us (3%)
    pallas_call x1, Pallas kernels, on_device(): pl.pallas_call(move_kernel, out_shape=(jax.ShapeDtypeStruct((2, 4, 2, ROU...  252 us
    pallas_call x1, Pallas kernels, on_device(): pl.pallas_call(functools.partial(attend_kernel, math.gcd(512, token_local...  93.9 us
    pallas_call x1, Pallas kernels, on_device(): pl.pallas_call(project_kernel, out_shape=(taken,) * 3 + (jax.ShapeDtypeSt...  67.9 us

profile of v2, /device:TPU:0, one launch (start us, length us, event | category | flops | bytes accessed | tf_op | source)
XLA Modules:
  0.0 449.6 jit_solution(2483664318562485536)
XLA Ops:
  0.0 0.0 copy-start
  0.0 1.0 select_reduce_fusion.1
  1.0 1.2 select_reduce_fusion
  2.2 0.0 copy-start.4
  2.2 3.7 convert_reduce_fusion
  6.0 0.0 copy-start.3
  6.0 0.0 copy-done.2
  6.0 1.8 fusion.2
  7.8 0.0 copy-done.4
  7.9 0.4 fusion.6
  8.4 1.0 copy.25
  9.4 0.0 copy-done.3
  9.4 0.8 convolution_convert_fusion
  10.2 1.6 copy.27
  11.8 4.4 reshape.73.text
  16.3 9.1 %fusion.5 = bf16[2,512,3072]{2,1,0:T(8,128)(2,1)} fusion(bf16[2,512,3072]{2,1,0:T(8,128)(2,1)} %param.10, f32[2,3072]{1,0:T(2,128)S(1)} %get-tuple-element.21, f32[2,512]{1,0:T(2,128)S(1)} %add_rsqrt_fusion, f32[2,512]{1,0:T(2,128)S(1)} %broadcast_multiply_fusion, f32[2,3072]{1,0:T(2,128)S(1)} %get-tuple-element.22), kind=kLoop, calls=%fused_computation.7 | loop fusion | flops 18874368 | bytes 12640256 | tf_op jit(solution)/shard_map/convert_element_type | solution.py:19
  25.4 251.9 %move_tokens.1 = (bf16[2,4,2,4,64,3072]{5,4,3,2,1,0:T(8,128)(2,1)}, bf16[4,4,2,64,768]{4,3,2,1,0:T(8,128)(2,1)}, bf16[4,2,64,1536]{3,2,1,0:T(8,128)(2,1)}) custom-call(bf16[2,2,4,64,3072]{4,3,2,1,0:T(8,128)(2,1)} %bitcast.19, bf16[2,4,64,768]{3,2,1,0:T(8,128)(2,1)} %bitcast.21, bf16[2,4,64,1536]{3,2,1,0:T(8,128)(2,1)} %bitcast.20), custom_call_target="tpu_custom_call" | custom-call | tf_op jit(solution)/shard_map/move_tokens/pallas_call | solution.py:478
  277.3 2.5 reduce_sum.65.up
  279.8 2.5 reduce_sum.64
  282.3 1.0 copy.32
  283.3 67.9 %project.1 = (bf16[2,2048,512]{2,1,0:T(8,128)(2,1)}, bf16[2,2048,512]{2,1,0:T(8,128)(2,1)}, bf16[2,2048,512]{2,1,0:T(8,128)(2,1)}, bf16[2,4,128,1024]{3,2,1,0:T(8,128)(2,1)}) custom-call(bf16[2,2048,3072]{2,1,0:T(8,128)(2,1)} %bitcast.18, bf16[3072,1536]{1,0:T(8,128)(2,1)} %weight.1, bf16[2,64,3072]{2,1,0:T(8,128)(2,1)} %bitcast.23, ...), custom_call_target="tpu_custom_call" | custom-call | tf_op jit(solution)/shard_map/project/pallas_call | solution.py:503
  351.2 0.0 copy-start.1
  351.2 93.9 %attend.1 = bf16[8,512,512]{2,1,0:T(8,128)(2,1)} custom-call(bf16[2,2048,512]{2,1,0:T(8,128)(2,1)} %get-tuple-element.15.q, bf16[2,2048,512]{2,1,0:T(8,128)(2,1)} %get-tuple-element.16.k, bf16[2,2048,512]{2,1,0:T(8,128)(2,1)} %get-tuple-element.17.v, bf16[2,512,1024]{2,1,0:T(8,128)(2,1)} %bitcast.24), custom_call_target="tpu_custom_call" | custom-call | tf_op jit(solution)/shard_map/attend/pallas_call | solution.py:529
  445.1 4.5 copy.40
  (10 shorter events, 0.2 us)
Async XLA Ops:
  0.0 7.9 %copy-start = (bf16[4,3072,64]{1,2,0:T(8,128)(2,1)S(1)}, bf16[4,3072,64]{1,2,0:T(8,128)(2,1)}, u32[]{:S(2)}) copy-start(bf16[4,3072,64]{1,2,0:T(8,128)(2,1)} %param.13) | copy-start | bytes 4718596
  0.0 6.0 %copy-start.2 = (bf16[2,512,3072]{2,1,0:T(8,128)(2,1)S(1)}, bf16[2,512,3072]{2,1,0:T(8,128)(2,1)}, u32[]{:S(2)}) copy-start(bf16[2,512,3072]{2,1,0:T(8,128)(2,1)} %param.10) | copy-start | bytes 18874372
  2.2 5.6 %copy-start.4 = (f32[2,2,3072]{2,1,0:T(2,128)S(1)}, f32[2,2,3072]{2,1,0:T(2,128)}, u32[]{:S(2)}) copy-start(f32[2,2,3072]{2,1,0:T(2,128)} %param.11) | copy-start | bytes 147460
  6.0 3.5 copy-start.3
  351.2 98.4 %copy-start.1 = (bf16[4,3072,64]{1,2,0:T(8,128)(2,1)S(1)}, bf16[4,3072,64]{1,2,0:T(8,128)(2,1)}, u32[]{:S(2)}) copy-start(bf16[4,3072,64]{1,2,0:T(8,128)(2,1)} %param.13) | copy-start | bytes 4718596
